TPU v7x, 32 devices: a whole 2x2x4 slice. The times are simulated.
32 devices in a mesh: ctx: 2 (over x), hs: 16 (over z, y, core).
Axes of the slice: x: 2, y: 2, z: 4, core: 2. Of those that a mesh axis runs over, the one named last changes fastest.
Arguments:
- key_rows: bfloat16 [16, 1024, 512], P('hs', 'ctx'), may hold values from -6 to 6
- value_rows: bfloat16 [16, 1024, 512], P('hs', 'ctx'), may hold values from -6 to 6
- query_rows: bfloat16 [16, 1024, 512], P('hs', 'ctx'), may hold values from -6 to 6
- step_rates: float32 [16, 1024], P('hs', 'ctx'), may hold values from 0.0003 to 0.003
- fast_gate: bfloat16 [16, 512, 512], P('hs', 'ctx'), may hold values from -0.25 to 0.25
- fast_up: bfloat16 [16, 512, 512], P('hs', 'ctx'), may hold values from -0.25 to 0.25
- fast_down: bfloat16 [16, 512, 512], P('hs', 'ctx'), may hold values from -0.25 to 0.25
- out_gain: float32 [2048], replicated, may hold values from 0.1 to 1.9
- gate_input: bfloat16 [1024, 4, 2048], P(('ctx', 'hs')), may hold values from -6 to 6
- out_weight: bfloat16 [2048, 1024], P('hs'), may hold values from -0.125 to 0.125
Outputs:
- layer_out: bfloat16 [1024, 4, 1024], P(('ctx', 'hs'))
All inputs are finite; a program needn't handle non-finite values.
Results may differ from a plain program's by a relative error of at most 0.01.
Values may be sent and summed in bfloat16 or wider, within the bound.
A program may use at most 64 MiB of HBM per device.

v0:
```python
import functools

import jax
import jax.numpy as jnp
from jax import lax
from jax.experimental import pallas as pl
from jax.experimental.pallas import tpu as pltpu
from jax.sharding import PartitionSpec as P

epsilon = 1e-06


def rescale_rows(weight, update):
    base = weight.astype(jnp.float32)
    moved = base + update
    factor = jnp.sqrt(jnp.mean(base * base, -1, keepdims=True) + epsilon) / jnp.sqrt(
        jnp.mean(moved * moved, -1, keepdims=True) + epsilon
    )
    return (moved * factor).astype(jnp.bfloat16)


def inner_rows(left, right):
    return lax.dot_general(
        left, right, (((0,), (0,)), ((), ())), preferred_element_type=jnp.float32
    )


def body(
    key_rows,
    value_rows,
    query_rows,
    step_rates,
    fast_gate,
    fast_up,
    fast_down,
    out_gain,
    gate_input,
    out_weight,
):
    key_row = key_rows[0]
    value_row = value_rows[0]
    query_row = query_rows[0]
    rate_row = step_rates[0]
    whole_gate, whole_up, whole_down = (
        lax.all_gather(fast_gate, "ctx", axis=1, tiled=True),
        lax.all_gather(fast_up, "ctx", axis=1, tiled=True),
        lax.all_gather(fast_down, "ctx", axis=1, tiled=True),
    )
    gate_fast = whole_gate[0]
    up_fast = whole_up[0]
    down_fast = whole_down[0]
    pre_gate = jnp.dot(key_row, gate_fast.T, preferred_element_type=jnp.float32)
    pre_up = jnp.dot(key_row, up_fast.T, preferred_element_type=jnp.float32)
    sig_gate = jax.nn.sigmoid(pre_gate)
    act_gate = pre_gate * sig_gate
    hidden = (act_gate * pre_up).astype(jnp.bfloat16)
    scaled = (rate_row[:, None] * value_row.astype(jnp.float32)).astype(jnp.bfloat16)
    grad_down = inner_rows(scaled, hidden)
    back_hidden = jnp.dot(scaled, down_fast, preferred_element_type=jnp.float32)
    back_gate = (back_hidden * pre_up * sig_gate * (1.0 + pre_gate * (1.0 - sig_gate))).astype(
        jnp.bfloat16
    )
    back_up = (back_hidden * act_gate).astype(jnp.bfloat16)
    grad_gate = inner_rows(back_gate, key_row)
    grad_up = inner_rows(back_up, key_row)
    grad_gate, grad_up, grad_down = (
        lax.psum_scatter(grad_gate, "ctx", scatter_dimension=0, tiled=True),
        lax.psum_scatter(grad_up, "ctx", scatter_dimension=0, tiled=True),
        lax.psum_scatter(grad_down, "ctx", scatter_dimension=0, tiled=True),
    )
    part_gate = rescale_rows(fast_gate[0], grad_gate)
    part_up = rescale_rows(fast_up[0], grad_up)
    part_down = rescale_rows(fast_down[0], grad_down)
    new_gate, new_up, new_down = (
        lax.all_gather(part_gate, "ctx", axis=0, tiled=True),
        lax.all_gather(part_up, "ctx", axis=0, tiled=True),
        lax.all_gather(part_down, "ctx", axis=0, tiled=True),
    )
    query_gate = jnp.dot(query_row, new_gate.T, preferred_element_type=jnp.float32)
    query_up = jnp.dot(query_row, new_up.T, preferred_element_type=jnp.float32)
    query_hidden = (jax.nn.silu(query_gate) * query_up).astype(jnp.bfloat16)
    head_out = jnp.dot(query_hidden, new_down.T, preferred_element_type=jnp.float32).astype(
        jnp.bfloat16
    )
    width_hs = lax.axis_size("hs")
    head_size = head_out.shape[1]
    token_count = head_out.shape[0] // width_hs
    blocks = head_out.reshape(width_hs, token_count, head_size)
    moved = lax.all_to_all(blocks, "hs", split_axis=0, concat_axis=2, tiled=True)
    seq_count = gate_input.shape[1]
    model_width = gate_input.shape[2]
    head_count = model_width // head_size
    mixed = moved.reshape(token_count, seq_count, head_count, head_size).astype(jnp.float32)
    square = jnp.mean(mixed * mixed, -1, keepdims=True)
    scaled_heads = mixed * lax.rsqrt(square + epsilon) * out_gain.reshape(head_count, head_size)
    normed = (
        scaled_heads.reshape(token_count, seq_count, model_width)
        * jax.nn.silu(gate_input.astype(jnp.float32))
    ).astype(jnp.bfloat16)
    flat_rows = normed.reshape(token_count * seq_count, model_width)
    out_cols = out_weight.shape[1]
    full_weight = lax.all_gather(out_weight, "hs", axis=0, tiled=True)
    result = jnp.dot(flat_rows, full_weight, preferred_element_type=jnp.float32)
    return result.astype(jnp.bfloat16).reshape(token_count, seq_count, out_cols)


MESH = pl.DeviceIdType.MESH


def inner_cols(left, right):
    return lax.dot_general(
        left, right, (((1,), (1,)), ((), ())), preferred_element_type=jnp.float32
    )


def layer_kernel(
    layers,
    pieces,
    gate_hbm,
    up_hbm,
    down_hbm,
    key_hbm,
    value_hbm,
    query_hbm,
    side_hbm,
    weight_hbm,
    rate_ref,
    gain_ref,
    out_ref,
    fast,
    fresh,
    keys,
    values,
    rates,
    queries,
    side,
    opened,
    full,
    grads,
    heads,
    mixed,
    normed,
    laid,
    local_sem,
    ctx_send,
    ctx_recv,
    full_send,
    full_recv,
    head_send,
    head_recv,
    fresh_send,
    fresh_recv,
):
    ctx = lax.axis_index("ctx")
    me = lax.axis_index("hs")
    other = 1 - ctx
    count = 4 * layers
    depth, inner = me // 4, me % 4
    row, core = inner // 2, inner % 2
    row_peer = depth * 4 + (1 - row) * 2 + core
    core_peer = depth * 4 + row * 2 + (1 - core)
    pair = depth * 4 + row * 2 + ctx
    owner = core == ctx
    helper = core != ctx

    def remote(source, target, send, recv, device):
        return pltpu.make_async_remote_copy(
            src_ref=source,
            dst_ref=target,
            send_sem=send,
            recv_sem=recv,
            device_id=device,
            device_id_type=MESH,
        )

    part = gate_hbm.shape[1]
    tokens = key_hbm.shape[1]
    piece = tokens // pieces
    shard = weight_hbm.shape[0]

    def rows(start, size):
        return pl.ds(pl.multiple_of(start, size), size)

    weights = (gate_hbm, up_hbm, down_hbm)
    local = []
    for i, source in enumerate(weights):
        local.append(
            pltpu.make_async_copy(source.at[0], fast.at[i, rows(ctx * part, part)], local_sem.at[i])
        )
    local.append(
        pltpu.make_async_copy(key_hbm.at[0], keys.at[rows(ctx * tokens, tokens)], local_sem.at[3])
    )
    local.append(
        pltpu.make_async_copy(value_hbm.at[0], values.at[rows(ctx * tokens, tokens)], local_sem.at[4])
    )
    local.append(pltpu.make_async_copy(weight_hbm, full.at[rows(me * shard, shard)], local_sem.at[5]))
    local.append(pltpu.make_async_copy(query_hbm.at[0], queries, local_sem.at[6]))
    local.append(pltpu.make_async_copy(side_hbm, side, local_sem.at[7]))
    owned = [0, 1, 2, 3, 4, 6]
    for i in (5, 7):
        local[i].start()

    @pl.when(owner)
    def _():
        for i in owned:
            local[i].start()

    barrier = pltpu.get_barrier_semaphore()
    pl.semaphore_signal(barrier, inc=1, device_id={"ctx": other}, device_id_type=MESH)
    for step in range(1, count):
        for side_ctx in (ctx, other):
            pl.semaphore_signal(
                barrier,
                inc=1,
                device_id={"ctx": side_ctx, "hs": (me + step) % count},
                device_id_type=MESH,
            )
    pl.semaphore_wait(barrier, 2 * count - 1)

    swaps = []
    for i, source in enumerate(weights):
        swaps.append((source.at[0], lambda who, i=i: fast.at[i, rows(who * part, part)]))
    for j in range(pieces):
        for source, target in ((key_hbm.at[0], keys), (value_hbm.at[0], values)):
            swaps.append(
                (
                    source.at[pl.ds(j * piece, piece)],
                    lambda who, target=target, j=j: target.at[
                        rows(who * tokens + j * piece, piece)
                    ],
                )
            )
    swaps.append((rate_ref, lambda who: rates))
    outgoing = [
        remote(source, target(ctx), ctx_send.at[i], ctx_recv.at[i], {"ctx": other})
        for i, (source, target) in enumerate(swaps)
    ]
    incoming = [
        remote(source, target(other), ctx_send.at[i], ctx_recv.at[i], {"ctx": other})
        for i, (source, target) in enumerate(swaps)
    ]
    block_rows = tokens // count
    step_rows = 4 * block_rows
    mid = layers // 2
    near = (depth // mid) * mid
    order = [mid - near + (depth + step) % mid for step in range(mid)]
    order += [near + (depth + step) % mid for step in range(1, mid)] + [depth]
    asked = []
    for step in range(layers):
        span = rows(order[step] * step_rows, step_rows)
        slot = len(swaps) + step
        asked.append(
            remote(
                query_hbm.at[0, span],
                queries.at[span],
                ctx_send.at[slot],
                ctx_recv.at[slot],
                {"ctx": other, "hs": core_peer},
            )
        )

    @pl.when(helper)
    def _():
        for copy in outgoing[-1:] + outgoing[:-1] + asked:
            copy.start()

    def full_copy(source, index, slot, device):
        return remote(
            source,
            full.at[rows(index * shard, shard)],
            full_send.at[slot],
            full_recv.at[index],
            {"hs": device},
        )

    def arrived(index):
        block = full.at[rows(index * shard, shard)]
        remote(block, block, full_send.at[0], full_recv.at[index], {"hs": core_peer}).wait_recv()

    def held(index):
        return full.at[rows(index * shard, shard)]

    sends = [
        (depth < layers - 1, full_copy(weight_hbm, me, 0, me + 4)),
        (depth > 0, full_copy(weight_hbm, me, 1, me - 4)),
        (None, full_copy(weight_hbm, me, 2, row_peer)),
        (None, full_copy(weight_hbm, me, 3, core_peer)),
    ]

    def guarded(condition, action):
        if condition is None:
            action()
        else:
            pl.when(condition)(action)

    for condition, copy in sends:
        guarded(condition, copy.start)

    def relay(hop):
        for turn, (exists, onward) in enumerate(
            (
                (depth >= hop, depth < layers - 1),
                (depth + hop <= layers - 1, depth > 0),
            )
        ):
            index = me - 4 * hop if turn == 0 else me + 4 * hop
            slot = 4 + ((hop - 1) * 2 + turn) * 3
            next_device = me + 4 if turn == 0 else me - 4
            made = [
                (exists & onward, full_copy(held(index), index, slot, next_device)),
                (exists, full_copy(held(index), index, slot + 1, row_peer)),
                (exists, full_copy(held(index), index, slot + 2, core_peer)),
            ]
            pl.when(exists)(functools.partial(arrived, index))
            for condition, copy in made:
                guarded(condition, copy.start)
            sends.extend(made)

    crossed = []
    for step in range(layers):
        index = ((depth + step) % layers) * 4 + (1 - row) * 2 + core
        slot = 4 + 6 * (layers - 1) + step
        crossed.append((index, full_copy(held(index), index, slot, core_peer)))

    def cross():
        for index, copy in crossed:
            arrived(index)
            copy.start()

    def learn(start, rate, first):
        key_part = keys[rows(start, piece), :]
        rate_column = jnp.broadcast_to(rate, (128, piece)).T[:, :1]
        scaled_part = (rate_column * values[rows(start, piece), :].astype(jnp.float32)).astype(
            jnp.bfloat16
        )
        pre_gate = inner_cols(key_part, fast[0])
        pre_up = inner_cols(key_part, fast[1])
        sig_gate = jax.nn.sigmoid(pre_gate)
        act_gate = pre_gate * sig_gate
        hidden = (act_gate * pre_up).astype(jnp.bfloat16)
        back_hidden = jnp.dot(scaled_part, fast[2], preferred_element_type=jnp.float32)
        back_gate = (
            back_hidden * pre_up * sig_gate * (1.0 + pre_gate * (1.0 - sig_gate))
        ).astype(jnp.bfloat16)
        back_up = (back_hidden * act_gate).astype(jnp.bfloat16)
        terms = (
            inner_rows(back_gate, key_part),
            inner_rows(back_up, key_part),
            inner_rows(scaled_part, hidden),
        )
        for i, term in enumerate(terms):
            grads[i] = term if first else grads[i] + term

    handed = [
        remote(fresh.at[i], fresh.at[i], fresh_send.at[i], fresh_recv.at[i], {"hs": core_peer})
        for i in range(3)
    ]
    local[7].wait()
    gate = side[...].astype(jnp.float32)
    opened[...] = gate * jax.nn.sigmoid(gate)
    hops = list(range(1, layers))
    if hops:
        relay(hops.pop(0))

    @pl.when(owner)
    def _():
        for i in owned[:5]:
            local[i].wait()
        for copy in incoming[:3]:
            copy.wait_recv()
        for j in range(pieces):
            learn(ctx * tokens + j * piece, rate_ref[:, j * piece : (j + 1) * piece], j == 0)

    for j in range(pieces):
        if hops:
            relay(hops.pop(0))

        @pl.when(owner)
        def _():
            if j == 0:
                incoming[-1].wait_recv()
            incoming[3 + 2 * j].wait_recv()
            incoming[4 + 2 * j].wait_recv()
            learn(other * tokens + j * piece, rates[:, j * piece : (j + 1) * piece], False)

    for hop in hops:
        relay(hop)

    @pl.when(owner)
    def _():
        for i in range(3):
            fresh[i] = rescale_rows(fast[i], grads[i])
            handed[i].start()
        local[6].wait()

    @pl.when(helper)
    def _():
        cross()
        for copy in handed:
            copy.wait_recv()

    copies = []
    for step in range(1, layers + 1):
        target = order[step - 1]
        pl.when(helper)(asked[step - 1].wait_recv)
        query_part = queries[rows(target * step_rows, step_rows), :]
        query_gate = inner_cols(query_part, fresh[0])
        query_up = inner_cols(query_part, fresh[1])
        query_hidden = (query_gate * jax.nn.sigmoid(query_gate) * query_up).astype(jnp.bfloat16)
        head_part = inner_cols(query_hidden, fresh[2]).astype(jnp.bfloat16)
        heads[rows(target * step_rows, step_rows), :] = head_part
        for i in range(4):
            device = target * 4 + (inner + i) % 4
            source = heads.at[rows(device * block_rows, block_rows)]
            slot = len(copies)
            copy = remote(
                source,
                mixed.at[pair],
                head_send.at[slot],
                head_recv.at[pair],
                {"ctx": core, "hs": device},
            )
            condition = None
            if step == layers and i == 0:
                condition = helper

                @pl.when(owner)
                def _():
                    mixed[me] = source[...]

            guarded(condition, copy.start)
            copies.append((condition, copy))

    pl.when(owner)(cross)
    local[5].wait()
    for step in range(layers):
        for other_row in range(2):
            arrived(((depth + step) % layers) * 4 + ((row + other_row) % 2) * 2 + (1 - core))

    def head_arrived(index):
        remote(
            heads.at[pl.ds(0, block_rows)],
            mixed.at[index],
            head_send.at[0],
            head_recv.at[index],
            {"hs": core_peer},
        ).wait_recv()

    for step in range(1, count):
        head_arrived((me + step) % count)
    pl.when(helper)(functools.partial(head_arrived, me))

    for condition, copy in sends + copies:
        guarded(condition, copy.wait_send)
    for _, copy in crossed:
        copy.wait_send()

    @pl.when(helper)
    def _():
        for copy in outgoing + asked:
            copy.wait_send()

    @pl.when(owner)
    def _():
        for copy in handed:
            copy.wait_send()

    size = mixed.shape[2]
    head_count = side.shape[2] // size
    for seq in range(side.shape[1]):
        for head in range(head_count):
            columns = slice(head * size, (head + 1) * size)
            value = mixed[seq * head_count + head].astype(jnp.float32)
            square = jnp.mean(value * value, -1, keepdims=True)
            value = value * lax.rsqrt(square + epsilon) * gain_ref[:, columns]
            normed[seq * block_rows : (seq + 1) * block_rows, columns] = (
                value * opened[:, seq, columns]
            ).astype(jnp.bfloat16)
    result = jnp.dot(normed[...], full[...], preferred_element_type=jnp.float32)
    for seq in range(side.shape[1]):
        laid[:, seq, :] = result[seq * block_rows : (seq + 1) * block_rows]
    out_ref[...] = laid[...].astype(jnp.bfloat16)


def swapped_body(
    key_rows,
    value_rows,
    query_rows,
    step_rates,
    fast_gate,
    fast_up,
    fast_down,
    out_gain,
    gate_input,
    out_weight,
):
    layers = lax.axis_size("hs") // 4
    count = 4 * layers
    pieces = 2
    tokens, size = key_rows.shape[1:]
    hidden_size = 2 * fast_gate.shape[1]
    block_rows, seq_count, width = gate_input.shape
    columns = out_weight.shape[1]
    anywhere = pl.BlockSpec(memory_space=pl.ANY)
    inside = pl.BlockSpec(memory_space=pltpu.VMEM)
    half = jnp.bfloat16
    return pl.pallas_call(
        functools.partial(layer_kernel, layers, pieces),
        out_shape=jax.ShapeDtypeStruct((block_rows, seq_count, columns), half),
        in_specs=[anywhere] * 8 + [inside] * 2,
        out_specs=inside,
        scratch_shapes=[
            pltpu.VMEM((3, hidden_size, size), half),
            pltpu.VMEM((3, hidden_size, size), half),
            pltpu.VMEM((2 * tokens, size), half),
            pltpu.VMEM((2 * tokens, size), half),
            pltpu.VMEM((1, tokens), jnp.float32),
            pltpu.VMEM((tokens, size), half),
            pltpu.VMEM((block_rows, seq_count, width), half),
            pltpu.VMEM((block_rows, seq_count, width), jnp.float32),
            pltpu.VMEM((width, columns), half),
            pltpu.VMEM((3, hidden_size, size), jnp.float32),
            pltpu.VMEM((tokens, size), half),
            pltpu.VMEM((count, block_rows, size), half),
            pltpu.VMEM((seq_count * block_rows, width), half),
            pltpu.VMEM((block_rows, seq_count, columns), jnp.float32),
            pltpu.SemaphoreType.DMA((8,)),
            pltpu.SemaphoreType.DMA((4 + 2 * pieces + layers,)),
            pltpu.SemaphoreType.DMA((4 + 2 * pieces + layers,)),
            pltpu.SemaphoreType.DMA((4 + 6 * (layers - 1) + layers,)),
            pltpu.SemaphoreType.DMA((count,)),
            pltpu.SemaphoreType.DMA((count,)),
            pltpu.SemaphoreType.DMA((count,)),
            pltpu.SemaphoreType.DMA((3,)),
            pltpu.SemaphoreType.DMA((3,)),
        ],
        compiler_params=pltpu.CompilerParams(
            collective_id=0, has_side_effects=True, vmem_limit_bytes=60 * 1024 * 1024
        ),
    )(
        fast_gate,
        fast_up,
        fast_down,
        key_rows,
        value_rows,
        query_rows,
        gate_input,
        out_weight,
        step_rates,
        out_gain[None],
    )

def solution(mesh):
    def step(*arrays):
        paired = mesh.shape["ctx"] == 2 and mesh.shape["hs"] % 8 == 0
        paired = paired and arrays[0].shape[0] == 1
        return (swapped_body if paired else body)(*arrays)

    return jax.shard_map(
        step,
        mesh=mesh,
        in_specs=(
            P("hs", "ctx", None),
            P("hs", "ctx", None),
            P("hs", "ctx", None),
            P("hs", "ctx"),
            P("hs", "ctx", None),
            P("hs", "ctx", None),
            P("hs", "ctx", None),
            P(),
            P(("ctx", "hs"), None, None),
            P("hs", None),
        ),
        out_specs=P(("ctx", "hs"), None, None),
        check_vma=False,
    )
```

profile of v0, /device:TPU:0, one launch (start us, length us, event | category | flops | bytes accessed | tf_op | source)
XLA Modules:
  0.0 48.5 jit_solution(1029923405943678039)
XLA Ops:
  0.0 46.8 %shard_map.100 = bf16[32,4,1024]{2,1,0:T(4,128)(2,1)} custom-call(bf16[1,256,512]{2,1,0:T(8,128)(2,1)} %gate_hbm.1, bf16[1,256,512]{2,1,0:T(8,128)(2,1)} %up_hbm.1, bf16[1,256,512]{2,1,0:T(8,128)(2,1)} %down_hbm.1, bf16[1,512,512]{2,1,0:T(8,128)(2,1)} %key_hbm.1, bf16[1,512,512]{2,1,0:T(8,128)(2,1)} %value_hbm.1, bf16[1,512,512]{2,1,0:T(8,128)(2,1)} %query_hbm.1, ...), custom_call_target="tpu_custom_call" | custom-call | tf_op jit(solution)/shard_map/pallas_call | solution.py:507
  46.8 1.7 %copy.12 = bf16[32,4,1024]{2,1,0:T(4,128)(2,1)} copy(bf16[32,4,1024]{2,1,0:T(4,128)(2,1)} %shard_map.100) | data formatting | bytes 524288
where the time goes:
time: 48.7 us; the launch traced here: 48.5 us
  Pallas kernels  46.8 us (96%)
  local copies, waits for them, and re-layouts  1.74 us (4%)
    pallas_call x1, Pallas kernels, swapped_body(): pl.pallas_call(functools.partial(layer_kernel, layers, pieces), out_shape...  46.8 us
    unnamed x1, local copies, waits for them, and re-layouts  1.74 us

commit v1 on v0

--- a/solution.py
+++ b/solution.py
@@ -150,6 +150,7 @@
     head_recv,
     fresh_send,
     fresh_recv,
+    ready,
 ):
     ctx = lax.axis_index("ctx")
     me = lax.axis_index("hs")
@@ -181,6 +182,12 @@
     def rows(start, size):
         return pl.ds(pl.multiple_of(start, size), size)
 
+    def guarded(condition, action):
+        if condition is None:
+            action()
+        else:
+            pl.when(condition)(action)
+
     weights = (gate_hbm, up_hbm, down_hbm)
     local = []
     for i, source in enumerate(weights):
@@ -205,17 +212,31 @@
         for i in owned:
             local[i].start()
 
+    last = layers - 1
+    links = [
+        (None, {"ctx": other}),
+        (None, {"hs": row_peer}),
+        (None, {"hs": core_peer}),
+        (depth < last, {"hs": me + 4}),
+        (depth > 0, {"hs": me - 4}),
+    ]
+    link_count = 3 + jnp.where(depth < last, 1, 0) + jnp.where(depth > 0, 1, 0)
+
+    def greet(semaphore):
+        for condition, device in links:
+            guarded(
+                condition,
+                functools.partial(
+                    pl.semaphore_signal, semaphore, inc=1, device_id=device, device_id_type=MESH
+                ),
+            )
+
     barrier = pltpu.get_barrier_semaphore()
-    pl.semaphore_signal(barrier, inc=1, device_id={"ctx": other}, device_id_type=MESH)
-    for step in range(1, count):
-        for side_ctx in (ctx, other):
-            pl.semaphore_signal(
-                barrier,
-                inc=1,
-                device_id={"ctx": side_ctx, "hs": (me + step) % count},
-                device_id_type=MESH,
-            )
-    pl.semaphore_wait(barrier, 2 * count - 1)
+    greet(barrier)
+    pl.semaphore_signal(
+        barrier, inc=1, device_id={"ctx": other, "hs": core_peer}, device_id_type=MESH
+    )
+    pl.semaphore_wait(barrier, link_count + 1)
 
     swaps = []
     for i, source in enumerate(weights):
@@ -287,14 +308,12 @@
         (None, full_copy(weight_hbm, me, 3, core_peer)),
     ]
 
-    def guarded(condition, action):
-        if condition is None:
-            action()
-        else:
-            pl.when(condition)(action)
-
     for condition, copy in sends:
         guarded(condition, copy.start)
+
+    for i in range(layers + 1):
+        greet(ready.at[i])
+        pl.semaphore_wait(ready.at[i], link_count)
 
     def relay(hop):
         for turn, (exists, onward) in enumerate(
@@ -533,6 +552,7 @@
             pltpu.SemaphoreType.DMA((count,)),
             pltpu.SemaphoreType.DMA((3,)),
             pltpu.SemaphoreType.DMA((3,)),
+            pltpu.SemaphoreType.REGULAR((layers + 1,)),
         ],
         compiler_params=pltpu.CompilerParams(
             collective_id=0, has_side_effects=True, vmem_limit_bytes=60 * 1024 * 1024

time: 48.7 us -> 48.4 us (level)
  the two profiles are of different devices: /device:TPU:0 before, /device:TPU:9 now
where the time goes in v1:
time: 48.4 us; the launch traced here: 48.2 us
  Pallas kernels  46.4 us (96%)
  local copies, waits for them, and re-layouts  1.74 us (4%)
    pallas_call x1, Pallas kernels, swapped_body(): pl.pallas_call(functools.partial(layer_kernel, layers, pieces), out_shape...  46.4 us
    unnamed x1, local copies, waits for them, and re-layouts  1.74 us

profile of v1, /device:TPU:9, one launch (start us, length us, event | category | flops | bytes accessed | tf_op | source)
XLA Modules:
  0.0 48.2 jit_solution(15484848590295881894)
XLA Ops:
  0.0 46.4 %shard_map.100 = bf16[32,4,1024]{2,1,0:T(4,128)(2,1)} custom-call(bf16[1,256,512]{2,1,0:T(8,128)(2,1)} %gate_hbm.1, bf16[1,256,512]{2,1,0:T(8,128)(2,1)} %up_hbm.1, bf16[1,256,512]{2,1,0:T(8,128)(2,1)} %down_hbm.1, bf16[1,512,512]{2,1,0:T(8,128)(2,1)} %key_hbm.1, bf16[1,512,512]{2,1,0:T(8,128)(2,1)} %value_hbm.1, bf16[1,512,512]{2,1,0:T(8,128)(2,1)} %query_hbm.1, ...), custom_call_target="tpu_custom_call" | custom-call | tf_op jit(solution)/shard_map/pallas_call | solution.py:526
  46.4 1.7 %copy.12 = bf16[32,4,1024]{2,1,0:T(4,128)(2,1)} copy(bf16[32,4,1024]{2,1,0:T(4,128)(2,1)} %shard_map.100) | data formatting | bytes 524288

commit v2 on v1

v2 whole, which is shorter than its diff:
```python
import functools

import jax
import jax.numpy as jnp
from jax import lax
from jax.experimental import pallas as pl
from jax.experimental.pallas import tpu as pltpu
from jax.sharding import PartitionSpec as P

epsilon = 1e-06


def rescale_rows(weight, update):
    base = weight.astype(jnp.float32)
    moved = base + update
    factor = jnp.sqrt(jnp.mean(base * base, -1, keepdims=True) + epsilon) / jnp.sqrt(
        jnp.mean(moved * moved, -1, keepdims=True) + epsilon
    )
    return (moved * factor).astype(jnp.bfloat16)


def inner_rows(left, right):
    return lax.dot_general(
        left, right, (((0,), (0,)), ((), ())), preferred_element_type=jnp.float32
    )


def body(
    key_rows,
    value_rows,
    query_rows,
    step_rates,
    fast_gate,
    fast_up,
    fast_down,
    out_gain,
    gate_input,
    out_weight,
):
    key_row = key_rows[0]
    value_row = value_rows[0]
    query_row = query_rows[0]
    rate_row = step_rates[0]
    whole_gate, whole_up, whole_down = (
        lax.all_gather(fast_gate, "ctx", axis=1, tiled=True),
        lax.all_gather(fast_up, "ctx", axis=1, tiled=True),
        lax.all_gather(fast_down, "ctx", axis=1, tiled=True),
    )
    gate_fast = whole_gate[0]
    up_fast = whole_up[0]
    down_fast = whole_down[0]
    pre_gate = jnp.dot(key_row, gate_fast.T, preferred_element_type=jnp.float32)
    pre_up = jnp.dot(key_row, up_fast.T, preferred_element_type=jnp.float32)
    sig_gate = jax.nn.sigmoid(pre_gate)
    act_gate = pre_gate * sig_gate
    hidden = (act_gate * pre_up).astype(jnp.bfloat16)
    scaled = (rate_row[:, None] * value_row.astype(jnp.float32)).astype(jnp.bfloat16)
    grad_down = inner_rows(scaled, hidden)
    back_hidden = jnp.dot(scaled, down_fast, preferred_element_type=jnp.float32)
    back_gate = (back_hidden * pre_up * sig_gate * (1.0 + pre_gate * (1.0 - sig_gate))).astype(
        jnp.bfloat16
    )
    back_up = (back_hidden * act_gate).astype(jnp.bfloat16)
    grad_gate = inner_rows(back_gate, key_row)
    grad_up = inner_rows(back_up, key_row)
    grad_gate, grad_up, grad_down = (
        lax.psum_scatter(grad_gate, "ctx", scatter_dimension=0, tiled=True),
        lax.psum_scatter(grad_up, "ctx", scatter_dimension=0, tiled=True),
        lax.psum_scatter(grad_down, "ctx", scatter_dimension=0, tiled=True),
    )
    part_gate = rescale_rows(fast_gate[0], grad_gate)
    part_up = rescale_rows(fast_up[0], grad_up)
    part_down = rescale_rows(fast_down[0], grad_down)
    new_gate, new_up, new_down = (
        lax.all_gather(part_gate, "ctx", axis=0, tiled=True),
        lax.all_gather(part_up, "ctx", axis=0, tiled=True),
        lax.all_gather(part_down, "ctx", axis=0, tiled=True),
    )
    query_gate = jnp.dot(query_row, new_gate.T, preferred_element_type=jnp.float32)
    query_up = jnp.dot(query_row, new_up.T, preferred_element_type=jnp.float32)
    query_hidden = (jax.nn.silu(query_gate) * query_up).astype(jnp.bfloat16)
    head_out = jnp.dot(query_hidden, new_down.T, preferred_element_type=jnp.float32).astype(
        jnp.bfloat16
    )
    width_hs = lax.axis_size("hs")
    head_size = head_out.shape[1]
    token_count = head_out.shape[0] // width_hs
    blocks = head_out.reshape(width_hs, token_count, head_size)
    moved = lax.all_to_all(blocks, "hs", split_axis=0, concat_axis=2, tiled=True)
    seq_count = gate_input.shape[1]
    model_width = gate_input.shape[2]
    head_count = model_width // head_size
    mixed = moved.reshape(token_count, seq_count, head_count, head_size).astype(jnp.float32)
    square = jnp.mean(mixed * mixed, -1, keepdims=True)
    scaled_heads = mixed * lax.rsqrt(square + epsilon) * out_gain.reshape(head_count, head_size)
    normed = (
        scaled_heads.reshape(token_count, seq_count, model_width)
        * jax.nn.silu(gate_input.astype(jnp.float32))
    ).astype(jnp.bfloat16)
    flat_rows = normed.reshape(token_count * seq_count, model_width)
    out_cols = out_weight.shape[1]
    full_weight = lax.all_gather(out_weight, "hs", axis=0, tiled=True)
    result = jnp.dot(flat_rows, full_weight, preferred_element_type=jnp.float32)
    return result.astype(jnp.bfloat16).reshape(token_count, seq_count, out_cols)


MESH = pl.DeviceIdType.MESH


def inner_cols(left, right):
    return lax.dot_general(
        left, right, (((1,), (1,)), ((), ())), preferred_element_type=jnp.float32
    )


def layer_kernel(
    layers,
    pieces,
    gate_hbm,
    up_hbm,
    down_hbm,
    key_hbm,
    value_hbm,
    query_hbm,
    side_hbm,
    weight_hbm,
    rate_hbm,
    gain_hbm,
    out_ref,
    fast,
    fresh,
    keys,
    values,
    rates,
    queries,
    gain,
    side,
    moved,
    gates,
    full,
    grads,
    heads,
    mixed,
    normed,
    outs,
    landed,
    laid,
    local_sem,
    ctx_send,
    ctx_recv,
    full_send,
    full_recv,
    gate_send,
    gate_recv,
    head_send,
    head_recv,
    out_send,
    out_recv,
    ready,
):
    ctx = lax.axis_index("ctx")
    me = lax.axis_index("hs")
    other = 1 - ctx
    count = 4 * layers
    last = layers - 1
    depth, inner = me // 4, me % 4
    row, core = inner // 2, inner % 2
    row_peer = depth * 4 + (1 - row) * 2 + core
    core_peer = depth * 4 + row * 2 + (1 - core)
    owner = core == ctx
    helper = core != ctx
    part = gate_hbm.shape[1]
    tokens = key_hbm.shape[1]
    piece = tokens // pieces
    shard = weight_hbm.shape[0]
    block_rows = tokens // count
    step_rows = 4 * block_rows
    seq_count = side.shape[1]
    size = key_hbm.shape[2]
    head_count = side.shape[2] // size

    def remote(source, target, send, recv, device):
        return pltpu.make_async_remote_copy(
            src_ref=source,
            dst_ref=target,
            send_sem=send,
            recv_sem=recv,
            device_id=device,
            device_id_type=MESH,
        )

    def rows(start, size):
        return pl.ds(pl.multiple_of(start, size), size)

    def guarded(condition, action):
        if condition is None:
            action()
        else:
            pl.when(condition)(action)

    links = [
        (None, {"ctx": other}),
        (None, {"hs": row_peer}),
        (None, {"hs": core_peer}),
        (depth < last, {"hs": me + 4}),
        (depth > 0, {"hs": me - 4}),
    ]
    link_count = 3 + jnp.where(depth < last, 1, 0) + jnp.where(depth > 0, 1, 0)

    def greet(semaphore):
        for condition, device in links:
            guarded(
                condition,
                functools.partial(
                    pl.semaphore_signal, semaphore, inc=1, device_id=device, device_id_type=MESH
                ),
            )

    barrier = pltpu.get_barrier_semaphore()
    greet(barrier)

    weights = (gate_hbm, up_hbm, down_hbm)
    near = rows(ctx * tokens, tokens)
    local = []
    for i, source in enumerate(weights):
        local.append((source.at[0], fast.at[i, rows(ctx * part, part)]))
    local.append((key_hbm.at[0], keys.at[near]))
    local.append((value_hbm.at[0], values.at[near]))
    local.append((query_hbm.at[0], queries.at[near]))
    local.append((rate_hbm, rates.at[ctx]))
    local.append((side_hbm, side))
    local.append((weight_hbm, full.at[rows(me * shard, shard)]))
    local.append((gain_hbm, gain))
    local = [
        pltpu.make_async_copy(source, target, local_sem.at[i])
        for i, (source, target) in enumerate(local)
    ]
    owned = local[:7]

    @pl.when(owner)
    def _():
        for copy in owned:
            copy.start()

    for copy in local[7:]:
        copy.start()
    pl.semaphore_wait(barrier, link_count)

    mid = layers // 2
    side_half = (depth // mid) * mid
    order = [mid - side_half + (depth + step) % mid for step in range(mid)]
    order += [side_half + (depth + step) % mid for step in range(1, mid)] + [depth]

    swaps = [(rate_hbm, lambda who: rates.at[who])]
    for i, source in enumerate(weights):
        swaps.append((source.at[0], lambda who, i=i: fast.at[i, rows(who * part, part)]))
    for j in range(pieces):
        for source, target in ((key_hbm.at[0], keys), (value_hbm.at[0], values)):
            swaps.append(
                (
                    source.at[pl.ds(j * piece, piece)],
                    lambda who, target=target, j=j: target.at[
                        rows(who * tokens + j * piece, piece)
                    ],
                )
            )
    for step in range(layers):
        swaps.append(
            (
                query_hbm.at[0, rows(order[step] * step_rows, step_rows)],
                lambda who, step=step: queries.at[
                    rows(who * tokens + order[step] * step_rows, step_rows)
                ],
            )
        )
    outgoing = [
        remote(source, target(ctx), ctx_send.at[i], ctx_recv.at[i], {"ctx": other})
        for i, (source, target) in enumerate(swaps)
    ]
    incoming = [
        remote(source, target(other), ctx_send.at[i], ctx_recv.at[i], {"ctx": other})
        for i, (source, target) in enumerate(swaps)
    ]
    asked = incoming[-layers:]

    def held(index):
        return full.at[rows(index * shard, shard)]

    used = []

    def full_copy(source, index, device):
        slot = len(used)
        used.append(slot)
        return remote(source, held(index), full_send.at[slot], full_recv.at[index], {"hs": device})

    def arrived(index):
        block = held(index)
        remote(block, block, full_send.at[0], full_recv.at[index], {"hs": core_peer}).wait_recv()

    def start_all(made):
        for condition, copy in made:
            guarded(condition, copy.start)

    first_sends = [
        (None, full_copy(weight_hbm, me, core_peer)),
        (depth < last, full_copy(weight_hbm, me, me + 4)),
        (depth > 0, full_copy(weight_hbm, me, me - 4)),
        (None, full_copy(weight_hbm, me, row_peer)),
    ]
    second_sends = [
        (depth < last, full_copy(held(core_peer), core_peer, me + 4)),
        (depth > 0, full_copy(held(core_peer), core_peer, me - 4)),
        (None, full_copy(held(core_peer), core_peer, row_peer)),
    ]
    relays = []
    for hop in range(1, layers):
        for base in (me, core_peer):
            for upward in (True, False):
                exists = depth >= hop if upward else depth + hop <= last
                onward = depth < last if upward else depth > 0
                index = base - 4 * hop if upward else base + 4 * hop
                next_device = me + 4 if upward else me - 4
                made = [
                    (exists & onward, full_copy(held(index), index, next_device)),
                    (exists, full_copy(held(index), index, row_peer)),
                    (exists, full_copy(held(index), index, core_peer)),
                ]
                relays.append((hop, exists, index, made))
    crossed = []
    for step in range(layers):
        for base in (row_peer, depth * 4 + (1 - row) * 2 + (1 - core)):
            index = (base + 4 * step) % count
            crossed.append((index, full_copy(held(index), index, core_peer)))

    own_copy = remote(
        weight_hbm, held(me), full_send.at[0], full_recv.at[me], {"hs": core_peer}
    )

    @pl.when(owner)
    def _():
        own_copy.start()

    @pl.when(helper)
    def _():
        for copy in outgoing:
            copy.start()
        start_all(first_sends)

    for i in range(max(2, layers - 2)):
        greet(ready.at[i])
        pl.semaphore_wait(ready.at[i], link_count)

    @pl.when(helper)
    def _():
        arrived(core_peer)
        start_all(second_sends)

    local[7].wait()
    spread = side[...].astype(jnp.float32)
    for seq in range(seq_count):
        moved[seq] = spread[:, seq, :].astype(jnp.bfloat16)
    gate_copies = [
        remote(
            moved.at[order[step]],
            gates.at[depth],
            gate_send.at[step],
            gate_recv.at[depth],
            {"hs": order[step] * 4 + inner},
        )
        for step in range(last)
    ]

    @pl.when(helper)
    def _():
        opened_hop = max(1, layers - 2)
        for position, (hop, exists, index, made) in enumerate(relays):
            pl.when(exists)(functools.partial(arrived, index))
            start_all(made)
            if hop == opened_hop and position + 1 == 4 * opened_hop:
                for copy in gate_copies:
                    copy.start()
        for index, copy in crossed:
            arrived(index)
            copy.start()

    def learn(start, rate, first):
        key_part = keys[rows(start, piece), :]
        rate_column = jnp.broadcast_to(rate, (128, piece)).T[:, :1]
        scaled_part = (rate_column * values[rows(start, piece), :].astype(jnp.float32)).astype(
            jnp.bfloat16
        )
        pre_gate = inner_cols(key_part, fast[0])
        pre_up = inner_cols(key_part, fast[1])
        sig_gate = jax.nn.sigmoid(pre_gate)
        act_gate = pre_gate * sig_gate
        hidden = (act_gate * pre_up).astype(jnp.bfloat16)
        back_hidden = jnp.dot(scaled_part, fast[2], preferred_element_type=jnp.float32)
        back_gate = (
            back_hidden * pre_up * sig_gate * (1.0 + pre_gate * (1.0 - sig_gate))
        ).astype(jnp.bfloat16)
        back_up = (back_hidden * act_gate).astype(jnp.bfloat16)
        terms = (
            inner_rows(back_gate, key_part),
            inner_rows(back_up, key_part),
            inner_rows(scaled_part, hidden),
        )
        for i, term in enumerate(terms):
            grads[i] = term if first else grads[i] + term

    head_copies = {}
    for half in (other, ctx):
        for step in range(layers):
            start = half * tokens + order[step] * step_rows
            for i in range(3 if half is ctx else 4):
                place = (inner + 1 + i) % 4
                head_copies[half is ctx, step, i] = remote(
                    heads.at[rows(start + place * block_rows, block_rows)],
                    mixed.at[order[step], row * 2 + ctx],
                    head_send.at[len(head_copies)],
                    head_recv.at[order[step], row * 2 + ctx],
                    {"ctx": half, "hs": depth * 4 + place},
                )

    def answer(half, step):
        target = order[step]
        start = half * tokens + target * step_rows
        query_part = queries[rows(start, step_rows), :]
        query_gate = inner_cols(query_part, fresh[0])
        query_up = inner_cols(query_part, fresh[1])
        query_hidden = (query_gate * jax.nn.sigmoid(query_gate) * query_up).astype(jnp.bfloat16)
        heads[rows(start, step_rows), :] = inner_cols(query_hidden, fresh[2]).astype(jnp.bfloat16)
        for i in range(4):
            if half is ctx and i == 3:
                mixed[target, row * 2 + ctx] = heads[
                    rows(start + inner * block_rows, block_rows), :
                ]
            else:
                head_copies[half is ctx, step, i].start()

    @pl.when(owner)
    def _():
        for i in (0, 1, 2, 3, 4, 6):
            local[i].wait()
        for copy in gate_copies:
            copy.start()
        for copy in incoming[1:4]:
            copy.wait_recv()
        for j in range(pieces):
            learn(ctx * tokens + j * piece, rates[ctx, :, j * piece : (j + 1) * piece], j == 0)
        incoming[0].wait_recv()
        for j in range(pieces):
            incoming[4 + 2 * j].wait_recv()
            incoming[5 + 2 * j].wait_recv()
            learn(
                other * tokens + j * piece, rates[other, :, j * piece : (j + 1) * piece], False
            )
        for i in range(3):
            fresh[i] = rescale_rows(fast[i], grads[i])
        local[5].wait()
        for step in range(layers):
            asked[step].wait_recv()
            answer(other, step)
            answer(ctx, step)
        for step in range(1, count):
            arrived((me + step) % count)

    local[8].wait()
    local[9].wait()

    def wait_head(target, slot):
        block = mixed.at[target, slot]
        remote(
            block, block, head_send.at[0], head_recv.at[target, slot], {"hs": core_peer}
        ).wait_recv()

    out_copies = []
    for step in range(layers):
        target = order[step]
        for i in range(3):
            wait_head(target, (row * 2 + ctx + 1 + i) % 4)
        pl.when(helper)(functools.partial(wait_head, target, row * 2 + ctx))
        if step < last:
            block = gates.at[target]
            remote(
                block, block, gate_send.at[0], gate_recv.at[target], {"hs": core_peer}
            ).wait_recv()
            opened = gates[target]
        else:
            opened = moved[depth]
        opened = opened.astype(jnp.float32)
        opened = opened * jax.nn.sigmoid(opened)
        for head in range(head_count):
            columns = slice(head * size, (head + 1) * size)
            value = mixed[target, head].astype(jnp.float32)
            square = jnp.mean(value * value, -1, keepdims=True)
            value = value * lax.rsqrt(square + epsilon) * gain[:, columns]
            normed[step, :, columns] = (value * opened[:, columns]).astype(jnp.bfloat16)
        result = jnp.dot(normed[step], full[...], preferred_element_type=jnp.float32)
        if step < last:
            outs[step] = result.astype(jnp.bfloat16)
            copy = remote(
                outs.at[step],
                landed.at[depth],
                out_send.at[step],
                out_recv.at[depth],
                {"hs": target * 4 + inner},
            )
            copy.start()
            out_copies.append(copy)
        else:
            landed[depth] = result.astype(jnp.bfloat16)

    @pl.when(owner)
    def _():
        own_copy.wait_send()
        for copy in head_copies.values():
            copy.wait_send()

    @pl.when(helper)
    def _():
        for copy in outgoing:
            copy.wait_send()
        for condition, copy in first_sends + second_sends:
            guarded(condition, copy.wait_send)
        for _, _, _, made in relays:
            for condition, copy in made:
                guarded(condition, copy.wait_send)
        for _, copy in crossed:
            copy.wait_send()

    for copy in gate_copies:
        copy.wait_send()
    for step in range(1, layers):
        source = (depth + step) % layers
        block = landed.at[source]
        remote(block, block, out_send.at[0], out_recv.at[source], {"hs": core_peer}).wait_recv()
    for copy in out_copies:
        copy.wait_send()
    for seq in range(seq_count):
        laid[:, seq, :] = landed[seq].astype(jnp.float32)
    out_ref[...] = laid[...].astype(jnp.bfloat16)


def swapped_body(
    key_rows,
    value_rows,
    query_rows,
    step_rates,
    fast_gate,
    fast_up,
    fast_down,
    out_gain,
    gate_input,
    out_weight,
):
    layers = lax.axis_size("hs") // 4
    count = 4 * layers
    pieces = 2
    tokens, size = key_rows.shape[1:]
    hidden_size = 2 * fast_gate.shape[1]
    block_rows, seq_count, width = gate_input.shape
    columns = out_weight.shape[1]
    anywhere = pl.BlockSpec(memory_space=pl.ANY)
    inside = pl.BlockSpec(memory_space=pltpu.VMEM)
    half = jnp.bfloat16
    dma = pltpu.SemaphoreType.DMA
    swaps = 4 + 2 * pieces + layers
    return pl.pallas_call(
        functools.partial(layer_kernel, layers, pieces),
        out_shape=jax.ShapeDtypeStruct((block_rows, seq_count, columns), half),
        in_specs=[anywhere] * 10,
        out_specs=inside,
        scratch_shapes=[
            pltpu.VMEM((3, hidden_size, size), half),
            pltpu.VMEM((3, hidden_size, size), half),
            pltpu.VMEM((2 * tokens, size), half),
            pltpu.VMEM((2 * tokens, size), half),
            pltpu.VMEM((2, 1, tokens), jnp.float32),
            pltpu.VMEM((2 * tokens, size), half),
            pltpu.VMEM((1, width), jnp.float32),
            pltpu.VMEM((block_rows, seq_count, width), half),
            pltpu.VMEM((seq_count, block_rows, width), half),
            pltpu.VMEM((layers, block_rows, width), half),
            pltpu.VMEM((width, columns), half),
            pltpu.VMEM((3, hidden_size, size), jnp.float32),
            pltpu.VMEM((2 * tokens, size), half),
            pltpu.VMEM((layers, 4, block_rows, size), half),
            pltpu.VMEM((layers, block_rows, width), half),
            pltpu.VMEM((layers, block_rows, columns), half),
            pltpu.VMEM((seq_count, block_rows, columns), half),
            pltpu.VMEM((block_rows, seq_count, columns), jnp.float32),
            dma((10,)),
            dma((swaps,)),
            dma((swaps,)),
            dma((7 + 12 * (layers - 1) + 2 * layers,)),
            dma((count,)),
            dma((layers,)),
            dma((layers,)),
            dma((8 * layers,)),
            dma((layers, 4)),
            dma((layers,)),
            dma((layers,)),
            pltpu.SemaphoreType.REGULAR((max(2, layers - 2),)),
        ],
        compiler_params=pltpu.CompilerParams(
            collective_id=0, has_side_effects=True, vmem_limit_bytes=60 * 1024 * 1024
        ),
    )(
        fast_gate,
        fast_up,
        fast_down,
        key_rows,
        value_rows,
        query_rows,
        gate_input,
        out_weight,
        step_rates,
        out_gain[None],
    )


def solution(mesh):
    def step(*arrays):
        paired = mesh.shape["ctx"] == 2 and mesh.shape["hs"] % 8 == 0
        paired = paired and arrays[0].shape[0] == 1
        paired = paired and arrays[8].shape[1] == mesh.shape["hs"] // 4
        paired = paired and arrays[8].shape[2] == 4 * arrays[0].shape[2]
        return (swapped_body if paired else body)(*arrays)

    return jax.shard_map(
        step,
        mesh=mesh,
        in_specs=(
            P("hs", "ctx", None),
            P("hs", "ctx", None),
            P("hs", "ctx", None),
            P("hs", "ctx"),
            P("hs", "ctx", None),
            P("hs", "ctx", None),
            P("hs", "ctx", None),
            P(),
            P(("ctx", "hs"), None, None),
            P("hs", None),
        ),
        out_specs=P(("ctx", "hs"), None, None),
        check_vma=False,
    )
```

time: 48.4 us -> 52.8 us (1.091)
  the two profiles are of different devices: /device:TPU:9 before, /device:TPU:0 now
where the time goes in v2:
time: 52.8 us; the launch traced here: 52.7 us
  Pallas kernels  50.9 us (96%)
  local copies, waits for them, and re-layouts  1.74 us (3%)
    pallas_call x1, Pallas kernels, swapped_body(): pl.pallas_call(functools.partial(layer_kernel, layers, pieces), out_shape...  50.9 us
    unnamed x1, local copies, waits for them, and re-layouts  1.74 us

profile of v2, /device:TPU:0, one launch (start us, length us, event | category | flops | bytes accessed | tf_op | source)
XLA Modules:
  0.0 52.7 jit_solution(11239851380812850146)
XLA Ops:
  0.0 50.9 %shard_map.100 = bf16[32,4,1024]{2,1,0:T(4,128)(2,1)} custom-call(bf16[1,256,512]{2,1,0:T(8,128)(2,1)} %gate_hbm.1, bf16[1,256,512]{2,1,0:T(8,128)(2,1)} %up_hbm.1, bf16[1,256,512]{2,1,0:T(8,128)(2,1)} %down_hbm.1, bf16[1,512,512]{2,1,0:T(8,128)(2,1)} %key_hbm.1, bf16[1,512,512]{2,1,0:T(8,128)(2,1)} %value_hbm.1, bf16[1,512,512]{2,1,0:T(8,128)(2,1)} %query_hbm.1, ...), custom_call_target="tpu_custom_call" | custom-call | tf_op jit(solution)/shard_map/pallas_call | solution.py:568
  50.9 1.7 %copy.12 = bf16[32,4,1024]{2,1,0:T(4,128)(2,1)} copy(bf16[32,4,1024]{2,1,0:T(4,128)(2,1)} %shard_map.100) | data formatting | bytes 524288

commit v3 on v2

--- a/solution.py
+++ b/solution.py
@@ -143,8 +143,6 @@
     mixed,
     normed,
     outs,
-    landed,
-    laid,
     local_sem,
     ctx_send,
     ctx_recv,
@@ -192,6 +190,9 @@
     def rows(start, size):
         return pl.ds(pl.multiple_of(start, size), size)
 
+    def drain(block, semaphore):
+        pltpu.make_async_copy(block, block, semaphore).wait()
+
     def guarded(condition, action):
         if condition is None:
             action()
@@ -221,28 +222,31 @@
 
     weights = (gate_hbm, up_hbm, down_hbm)
     near = rows(ctx * tokens, tokens)
-    local = []
-    for i, source in enumerate(weights):
-        local.append((source.at[0], fast.at[i, rows(ctx * part, part)]))
-    local.append((key_hbm.at[0], keys.at[near]))
-    local.append((value_hbm.at[0], values.at[near]))
-    local.append((query_hbm.at[0], queries.at[near]))
-    local.append((rate_hbm, rates.at[ctx]))
-    local.append((side_hbm, side))
-    local.append((weight_hbm, full.at[rows(me * shard, shard)]))
-    local.append((gain_hbm, gain))
-    local = [
-        pltpu.make_async_copy(source, target, local_sem.at[i])
-        for i, (source, target) in enumerate(local)
+    owned = [
+        pltpu.make_async_copy(source, target, local_sem.at[0])
+        for source, target in [
+            (source.at[0], fast.at[i, rows(ctx * part, part)])
+            for i, source in enumerate(weights)
+        ]
+        + [
+            (source.at[0], target.at[near])
+            for source, target in ((key_hbm, keys), (value_hbm, values), (query_hbm, queries))
+        ]
     ]
-    owned = local[:7]
+    own_rates = pltpu.make_async_copy(rate_hbm, rates.at[ctx], local_sem.at[1])
+    side_copy = pltpu.make_async_copy(side_hbm, side, local_sem.at[2])
+    own_shard = pltpu.make_async_copy(
+        weight_hbm, full.at[rows(me * shard, shard)], local_sem.at[3]
+    )
+    gain_copy = pltpu.make_async_copy(gain_hbm, gain, local_sem.at[4])
 
     @pl.when(owner)
     def _():
         for copy in owned:
             copy.start()
-
-    for copy in local[7:]:
+        own_rates.start()
+
+    for copy in (side_copy, own_shard, gain_copy):
         copy.start()
     pl.semaphore_wait(barrier, link_count)
 
@@ -273,25 +277,27 @@
                 ],
             )
         )
+    arrivals = [0, 1, 1, 1]
+    arrivals += [2 + j for j in range(pieces) for _ in range(2)]
+    arrivals += [2 + pieces + step for step in range(layers)]
     outgoing = [
-        remote(source, target(ctx), ctx_send.at[i], ctx_recv.at[i], {"ctx": other})
+        remote(
+            source,
+            target(ctx),
+            ctx_send.at[0 if i == 0 else 1],
+            ctx_recv.at[arrivals[i]],
+            {"ctx": other},
+        )
         for i, (source, target) in enumerate(swaps)
     ]
-    incoming = [
-        remote(source, target(other), ctx_send.at[i], ctx_recv.at[i], {"ctx": other})
-        for i, (source, target) in enumerate(swaps)
-    ]
-    asked = incoming[-layers:]
+    def lines(count):
+        return full.at[pl.ds(0, count * size // full.shape[1])]
 
     def held(index):
         return full.at[rows(index * shard, shard)]
 
-    used = []
-
-    def full_copy(source, index, device):
-        slot = len(used)
-        used.append(slot)
-        return remote(source, held(index), full_send.at[slot], full_recv.at[index], {"hs": device})
+    def full_copy(source, index, way, device):
+        return remote(source, held(index), full_send.at[way], full_recv.at[index], {"hs": device})
 
     def arrived(index):
         block = held(index)
@@ -302,15 +308,15 @@
             guarded(condition, copy.start)
 
     first_sends = [
-        (None, full_copy(weight_hbm, me, core_peer)),
-        (depth < last, full_copy(weight_hbm, me, me + 4)),
-        (depth > 0, full_copy(weight_hbm, me, me - 4)),
-        (None, full_copy(weight_hbm, me, row_peer)),
+        (None, full_copy(weight_hbm, me, 3, core_peer)),
+        (depth < last, full_copy(weight_hbm, me, 0, me + 4)),
+        (depth > 0, full_copy(weight_hbm, me, 1, me - 4)),
+        (None, full_copy(weight_hbm, me, 2, row_peer)),
     ]
     second_sends = [
-        (depth < last, full_copy(held(core_peer), core_peer, me + 4)),
-        (depth > 0, full_copy(held(core_peer), core_peer, me - 4)),
-        (None, full_copy(held(core_peer), core_peer, row_peer)),
+        (depth < last, full_copy(held(core_peer), core_peer, 0, me + 4)),
+        (depth > 0, full_copy(held(core_peer), core_peer, 1, me - 4)),
+        (None, full_copy(held(core_peer), core_peer, 2, row_peer)),
     ]
     relays = []
     for hop in range(1, layers):
@@ -321,19 +327,19 @@
                 index = base - 4 * hop if upward else base + 4 * hop
                 next_device = me + 4 if upward else me - 4
                 made = [
-                    (exists & onward, full_copy(held(index), index, next_device)),
-                    (exists, full_copy(held(index), index, row_peer)),
-                    (exists, full_copy(held(index), index, core_peer)),
+                    (exists & onward, full_copy(held(index), index, 0 if upward else 1, next_device)),
+                    (exists, full_copy(held(index), index, 2, row_peer)),
+                    (exists, full_copy(held(index), index, 3, core_peer)),
                 ]
                 relays.append((hop, exists, index, made))
     crossed = []
     for step in range(layers):
         for base in (row_peer, depth * 4 + (1 - row) * 2 + (1 - core)):
             index = (base + 4 * step) % count
-            crossed.append((index, full_copy(held(index), index, core_peer)))
+            crossed.append((index, full_copy(held(index), index, 3, core_peer)))
 
     own_copy = remote(
-        weight_hbm, held(me), full_send.at[0], full_recv.at[me], {"hs": core_peer}
+        weight_hbm, held(me), full_send.at[3], full_recv.at[me], {"hs": core_peer}
     )
 
     @pl.when(owner)
@@ -355,7 +361,7 @@
         arrived(core_peer)
         start_all(second_sends)
 
-    local[7].wait()
+    side_copy.wait()
     spread = side[...].astype(jnp.float32)
     for seq in range(seq_count):
         moved[seq] = spread[:, seq, :].astype(jnp.bfloat16)
@@ -363,7 +369,7 @@
         remote(
             moved.at[order[step]],
             gates.at[depth],
-            gate_send.at[step],
+            gate_send,
             gate_recv.at[depth],
             {"hs": order[step] * 4 + inner},
         )
@@ -416,8 +422,8 @@
                 head_copies[half is ctx, step, i] = remote(
                     heads.at[rows(start + place * block_rows, block_rows)],
                     mixed.at[order[step], row * 2 + ctx],
-                    head_send.at[len(head_copies)],
-                    head_recv.at[order[step], row * 2 + ctx],
+                    head_send,
+                    head_recv.at[order[step]],
                     {"ctx": half, "hs": depth * 4 + place},
                 )
 
@@ -439,51 +445,44 @@
 
     @pl.when(owner)
     def _():
-        for i in (0, 1, 2, 3, 4, 6):
-            local[i].wait()
-        for copy in gate_copies:
-            copy.start()
-        for copy in incoming[1:4]:
-            copy.wait_recv()
+        drain(lines(3 * part + 3 * tokens), local_sem.at[0])
+        own_rates.wait()
+        drain(lines(3 * part), ctx_recv.at[1])
         for j in range(pieces):
             learn(ctx * tokens + j * piece, rates[ctx, :, j * piece : (j + 1) * piece], j == 0)
-        incoming[0].wait_recv()
+        drain(rates.at[other], ctx_recv.at[0])
         for j in range(pieces):
-            incoming[4 + 2 * j].wait_recv()
-            incoming[5 + 2 * j].wait_recv()
+            drain(lines(2 * piece), ctx_recv.at[2 + j])
+            if j == 0:
+                for copy in gate_copies:
+                    copy.start()
             learn(
                 other * tokens + j * piece, rates[other, :, j * piece : (j + 1) * piece], False
             )
         for i in range(3):
             fresh[i] = rescale_rows(fast[i], grads[i])
-        local[5].wait()
         for step in range(layers):
-            asked[step].wait_recv()
+            drain(lines(step_rows), ctx_recv.at[2 + pieces + step])
             answer(other, step)
             answer(ctx, step)
         for step in range(1, count):
             arrived((me + step) % count)
 
-    local[8].wait()
-    local[9].wait()
-
-    def wait_head(target, slot):
-        block = mixed.at[target, slot]
-        remote(
-            block, block, head_send.at[0], head_recv.at[target, slot], {"hs": core_peer}
-        ).wait_recv()
-
-    out_copies = []
+    own_shard.wait()
+    gain_copy.wait()
     for step in range(layers):
         target = order[step]
-        for i in range(3):
-            wait_head(target, (row * 2 + ctx + 1 + i) % 4)
-        pl.when(helper)(functools.partial(wait_head, target, row * 2 + ctx))
+
+        @pl.when(owner)
+        def _():
+            drain(mixed.at[target, pl.ds(0, 3)], head_recv.at[target])
+
+        @pl.when(helper)
+        def _():
+            drain(mixed.at[target], head_recv.at[target])
+
         if step < last:
-            block = gates.at[target]
-            remote(
-                block, block, gate_send.at[0], gate_recv.at[target], {"hs": core_peer}
-            ).wait_recv()
+            drain(gates.at[target], gate_recv.at[target])
             opened = gates[target]
         else:
             opened = moved[depth]
@@ -496,49 +495,46 @@
             value = value * lax.rsqrt(square + epsilon) * gain[:, columns]
             normed[step, :, columns] = (value * opened[:, columns]).astype(jnp.bfloat16)
         result = jnp.dot(normed[step], full[...], preferred_element_type=jnp.float32)
+        outs[step] = result.astype(jnp.bfloat16)
         if step < last:
-            outs[step] = result.astype(jnp.bfloat16)
             copy = remote(
                 outs.at[step],
-                landed.at[depth],
-                out_send.at[step],
-                out_recv.at[depth],
+                out_ref.at[depth],
+                out_send,
+                out_recv,
                 {"hs": target * 4 + inner},
             )
-            copy.start()
-            out_copies.append(copy)
         else:
-            landed[depth] = result.astype(jnp.bfloat16)
+            copy = pltpu.make_async_copy(outs.at[step], out_ref.at[depth], local_sem.at[2])
+        copy.start()
 
     @pl.when(owner)
     def _():
-        own_copy.wait_send()
-        for copy in head_copies.values():
-            copy.wait_send()
+        drain(held(0), full_send.at[3])
+        drain(heads.at[pl.ds(0, 7 * layers * block_rows)], head_send)
+
+    def sent(amount, way):
+        if amount:
+            drain(full.at[pl.ds(0, amount * shard)], full_send.at[way])
 
     @pl.when(helper)
     def _():
-        for copy in outgoing:
-            copy.wait_send()
-        for condition, copy in first_sends + second_sends:
-            guarded(condition, copy.wait_send)
-        for _, _, _, made in relays:
-            for condition, copy in made:
-                guarded(condition, copy.wait_send)
-        for _, copy in crossed:
-            copy.wait_send()
-
-    for copy in gate_copies:
-        copy.wait_send()
-    for step in range(1, layers):
-        source = (depth + step) % layers
-        block = landed.at[source]
-        remote(block, block, out_send.at[0], out_recv.at[source], {"hs": core_peer}).wait_recv()
-    for copy in out_copies:
-        copy.wait_send()
-    for seq in range(seq_count):
-        laid[:, seq, :] = landed[seq].astype(jnp.float32)
-    out_ref[...] = laid[...].astype(jnp.bfloat16)
+        drain(rates.at[ctx], ctx_send.at[0])
+        drain(lines(3 * part + 3 * tokens), ctx_send.at[1])
+        for layer in range(layers):
+
+            @pl.when(depth == layer)
+            def _():
+                sent(2 + 2 * layer if layer < last else 0, 0)
+                sent(2 + 2 * (last - layer) if layer > 0 else 0, 1)
+
+        sent(2 * layers, 2)
+        sent(4 * layers - 1, 3)
+
+    drain(moved.at[pl.ds(0, last)], gate_send)
+    drain(outs.at[pl.ds(0, last)], out_send)
+    drain(outs.at[pl.ds(0, last)], out_recv)
+    drain(outs.at[0], local_sem.at[2])
 
 
 def swapped_body(
@@ -561,15 +557,13 @@
     block_rows, seq_count, width = gate_input.shape
     columns = out_weight.shape[1]
     anywhere = pl.BlockSpec(memory_space=pl.ANY)
-    inside = pl.BlockSpec(memory_space=pltpu.VMEM)
     half = jnp.bfloat16
     dma = pltpu.SemaphoreType.DMA
-    swaps = 4 + 2 * pieces + layers
-    return pl.pallas_call(
+    laid = pl.pallas_call(
         functools.partial(layer_kernel, layers, pieces),
-        out_shape=jax.ShapeDtypeStruct((block_rows, seq_count, columns), half),
+        out_shape=jax.ShapeDtypeStruct((seq_count, block_rows, columns), half),
         in_specs=[anywhere] * 10,
-        out_specs=inside,
+        out_specs=anywhere,
         scratch_shapes=[
             pltpu.VMEM((3, hidden_size, size), half),
             pltpu.VMEM((3, hidden_size, size), half),
@@ -587,19 +581,17 @@
             pltpu.VMEM((layers, 4, block_rows, size), half),
             pltpu.VMEM((layers, block_rows, width), half),
             pltpu.VMEM((layers, block_rows, columns), half),
-            pltpu.VMEM((seq_count, block_rows, columns), half),
-            pltpu.VMEM((block_rows, seq_count, columns), jnp.float32),
-            dma((10,)),
-            dma((swaps,)),
-            dma((swaps,)),
-            dma((7 + 12 * (layers - 1) + 2 * layers,)),
+            dma((5,)),
+            dma((2,)),
+            dma((2 + pieces + layers,)),
+            dma((4,)),
             dma((count,)),
+            dma(()),
             dma((layers,)),
+            dma(()),
             dma((layers,)),
-            dma((8 * layers,)),
-            dma((layers, 4)),
-            dma((layers,)),
-            dma((layers,)),
+            dma(()),
+            dma(()),
             pltpu.SemaphoreType.REGULAR((max(2, layers - 2),)),
         ],
         compiler_params=pltpu.CompilerParams(
@@ -617,6 +609,7 @@
         step_rates,
         out_gain[None],
     )
+    return laid.transpose(1, 0, 2)
 
 
 def solution(mesh):

time: 52.8 us -> 51 us (0.966)
  Pallas kernels: 50.9 us -> 49 us
    pallas_call x1, Pallas kernels: 50.9 us -> 49 us  [swapped_body(): pl.pallas_call(functools.partial(layer_kernel, layers, pieces), out_shape...]
    transpose x0 -> x1, local copies, waits for them, and re-layouts: none -> 1.86 us  [swapped_body(): return laid.transpose(1, 0, 2)]
    unnamed x1 -> x0, local copies, waits for them, and re-layouts: 1.74 us -> none
where the time goes in v3:
time: 51 us; the launch traced here: 50.9 us
  Pallas kernels  49 us (96%)
  local copies, waits for them, and re-layouts  1.86 us (4%)
    pallas_call x1, Pallas kernels, swapped_body(): pl.pallas_call(functools.partial(layer_kernel, layers, pieces), out_shape...  49 us
    transpose x1, local copies, waits for them, and re-layouts, swapped_body(): return laid.transpose(1, 0, 2)  1.86 us

profile of v3, /device:TPU:0, one launch (start us, length us, event | category | flops | bytes accessed | tf_op | source)
XLA Modules:
  0.0 50.9 jit_solution(13439506795380116857)
XLA Ops:
  0.0 49.0 %shard_map.100 = bf16[4,32,1024]{2,1,0:T(8,128)(2,1)} custom-call(bf16[1,256,512]{2,1,0:T(8,128)(2,1)} %gate_hbm.1, bf16[1,256,512]{2,1,0:T(8,128)(2,1)} %up_hbm.1, bf16[1,256,512]{2,1,0:T(8,128)(2,1)} %down_hbm.1, bf16[1,512,512]{2,1,0:T(8,128)(2,1)} %key_hbm.1, bf16[1,512,512]{2,1,0:T(8,128)(2,1)} %value_hbm.1, bf16[1,512,512]{2,1,0:T(8,128)(2,1)} %query_hbm.1, ...), custom_call_target="tpu_custom_call" | custom-call | tf_op jit(solution)/shard_map/pallas_call | solution.py:562
  49.0 1.9 %copy.11 = bf16[32,4,1024]{2,1,0:T(4,128)(2,1)} copy(bf16[32,4,1024]{2,0,1:T(8,128)(2,1)} %bitcast.2) | data formatting | bytes 524288 | tf_op jit(solution)/shard_map/transpose | solution.py:612

commit v4 on v3

--- a/solution.py
+++ b/solution.py
@@ -378,14 +378,13 @@
 
     @pl.when(helper)
     def _():
-        opened_hop = max(1, layers - 2)
         for position, (hop, exists, index, made) in enumerate(relays):
             pl.when(exists)(functools.partial(arrived, index))
             start_all(made)
-            if hop == opened_hop and position + 1 == 4 * opened_hop:
-                for copy in gate_copies:
-                    copy.start()
-        for index, copy in crossed:
+        for turn, (index, copy) in enumerate(crossed):
+            if turn == layers:
+                for gate_copy in gate_copies:
+                    gate_copy.start()
             arrived(index)
             copy.start()
 
@@ -453,7 +452,7 @@
         drain(rates.at[other], ctx_recv.at[0])
         for j in range(pieces):
             drain(lines(2 * piece), ctx_recv.at[2 + j])
-            if j == 0:
+            if j == pieces - 1:
                 for copy in gate_copies:
                     copy.start()
             learn(

time: 51 us -> 48.3 us (0.947)
  the two profiles are of different devices: /device:TPU:0 before, /device:TPU:4 now
where the time goes in v4:
time: 48.3 us; the launch traced here: 48.1 us
  Pallas kernels  46.2 us (96%)
  local copies, waits for them, and re-layouts  1.86 us (4%)
    pallas_call x1, Pallas kernels, swapped_body(): pl.pallas_call(functools.partial(layer_kernel, layers, pieces), out_shape...  46.2 us
    transpose x1, local copies, waits for them, and re-layouts, swapped_body(): return laid.transpose(1, 0, 2)  1.86 us

profile of v4, /device:TPU:4, one launch (start us, length us, event | category | flops | bytes accessed | tf_op | source)
XLA Modules:
  0.0 48.1 jit_solution(5468305808837272213)
XLA Ops:
  0.0 46.2 %shard_map.100 = bf16[4,32,1024]{2,1,0:T(8,128)(2,1)} custom-call(bf16[1,256,512]{2,1,0:T(8,128)(2,1)} %gate_hbm.1, bf16[1,256,512]{2,1,0:T(8,128)(2,1)} %up_hbm.1, bf16[1,256,512]{2,1,0:T(8,128)(2,1)} %down_hbm.1, bf16[1,512,512]{2,1,0:T(8,128)(2,1)} %key_hbm.1, bf16[1,512,512]{2,1,0:T(8,128)(2,1)} %value_hbm.1, bf16[1,512,512]{2,1,0:T(8,128)(2,1)} %query_hbm.1, ...), custom_call_target="tpu_custom_call" | custom-call | tf_op jit(solution)/shard_map/pallas_call | solution.py:561
  46.3 1.9 %copy.11 = bf16[32,4,1024]{2,1,0:T(4,128)(2,1)} copy(bf16[32,4,1024]{2,0,1:T(8,128)(2,1)} %bitcast.2) | data formatting | bytes 524288 | tf_op jit(solution)/shard_map/transpose | solution.py:611

commit v5 on v4

--- a/solution.py
+++ b/solution.py
@@ -376,15 +376,22 @@
         for step in range(last)
     ]
 
+    def start_gates(outermost):
+        for step, copy in enumerate(gate_copies):
+            target = order[step]
+            outer = (target == 0) | (target == last)
+            pl.when(outer if outermost else jnp.logical_not(outer))(copy.start)
+
     @pl.when(helper)
     def _():
         for position, (hop, exists, index, made) in enumerate(relays):
             pl.when(exists)(functools.partial(arrived, index))
             start_all(made)
+            if position + 1 == 4 * max(1, layers - 2):
+                start_gates(False)
         for turn, (index, copy) in enumerate(crossed):
             if turn == layers:
-                for gate_copy in gate_copies:
-                    gate_copy.start()
+                start_gates(True)
             arrived(index)
             copy.start()
 
@@ -449,12 +456,12 @@
         drain(lines(3 * part), ctx_recv.at[1])
         for j in range(pieces):
             learn(ctx * tokens + j * piece, rates[ctx, :, j * piece : (j + 1) * piece], j == 0)
+        start_gates(False)
         drain(rates.at[other], ctx_recv.at[0])
         for j in range(pieces):
             drain(lines(2 * piece), ctx_recv.at[2 + j])
             if j == pieces - 1:
-                for copy in gate_copies:
-                    copy.start()
+                start_gates(True)
             learn(
                 other * tokens + j * piece, rates[other, :, j * piece : (j + 1) * piece], False
             )

time: 48.3 us -> 46 us (0.952)
  the two profiles are of different devices: /device:TPU:4 before, /device:TPU:0 now
where the time goes in v5:
time: 46 us; the launch traced here: 45.8 us
  Pallas kernels  44 us (96%)
  local copies, waits for them, and re-layouts  1.86 us (4%)
    pallas_call x1, Pallas kernels, swapped_body(): pl.pallas_call(functools.partial(layer_kernel, layers, pieces), out_shape...  44 us
    transpose x1, local copies, waits for them, and re-layouts, swapped_body(): return laid.transpose(1, 0, 2)  1.86 us

profile of v5, /device:TPU:0, one launch (start us, length us, event | category | flops | bytes accessed | tf_op | source)
XLA Modules:
  0.0 45.8 jit_solution(18081590178538095511)
XLA Ops:
  0.0 44.0 %shard_map.100 = bf16[4,32,1024]{2,1,0:T(8,128)(2,1)} custom-call(bf16[1,256,512]{2,1,0:T(8,128)(2,1)} %gate_hbm.1, bf16[1,256,512]{2,1,0:T(8,128)(2,1)} %up_hbm.1, bf16[1,256,512]{2,1,0:T(8,128)(2,1)} %down_hbm.1, bf16[1,512,512]{2,1,0:T(8,128)(2,1)} %key_hbm.1, bf16[1,512,512]{2,1,0:T(8,128)(2,1)} %value_hbm.1, bf16[1,512,512]{2,1,0:T(8,128)(2,1)} %query_hbm.1, ...), custom_call_target="tpu_custom_call" | custom-call | tf_op jit(solution)/shard_map/pallas_call | solution.py:568
  44.0 1.9 %copy.11 = bf16[32,4,1024]{2,1,0:T(4,128)(2,1)} copy(bf16[32,4,1024]{2,0,1:T(8,128)(2,1)} %bitcast.2) | data formatting | bytes 524288 | tf_op jit(solution)/shard_map/transpose | solution.py:618

commit v6 on v5

--- a/solution.py
+++ b/solution.py
@@ -1,4 +1,5 @@
 import functools
+import math
 
 import jax
 import jax.numpy as jnp
@@ -188,7 +189,7 @@
         )
 
     def rows(start, size):
-        return pl.ds(pl.multiple_of(start, size), size)
+        return pl.ds(pl.multiple_of(start, math.gcd(size, 128)), size)
 
     def drain(block, semaphore):
         pltpu.make_async_copy(block, block, semaphore).wait()
@@ -278,8 +279,7 @@
             )
         )
     arrivals = [0, 1, 1, 1]
-    arrivals += [2 + j for j in range(pieces) for _ in range(2)]
-    arrivals += [2 + pieces + step for step in range(layers)]
+    arrivals += list(range(2, 2 + 2 * pieces + layers))
     outgoing = [
         remote(
             source,
@@ -395,29 +395,30 @@
             arrived(index)
             copy.start()
 
-    def learn(start, rate, first):
+    def forward(start):
         key_part = keys[rows(start, piece), :]
-        rate_column = jnp.broadcast_to(rate, (128, piece)).T[:, :1]
-        scaled_part = (rate_column * values[rows(start, piece), :].astype(jnp.float32)).astype(
-            jnp.bfloat16
-        )
         pre_gate = inner_cols(key_part, fast[0])
         pre_up = inner_cols(key_part, fast[1])
         sig_gate = jax.nn.sigmoid(pre_gate)
         act_gate = pre_gate * sig_gate
         hidden = (act_gate * pre_up).astype(jnp.bfloat16)
+        slope = pre_up * sig_gate * (1.0 + pre_gate * (1.0 - sig_gate))
+        return key_part, act_gate, hidden, slope
+
+    def backward(start, rate, made):
+        key_part, act_gate, hidden, slope = made
+        rate_column = jnp.broadcast_to(rate, (128, piece)).T[:, :1]
+        scaled_part = (rate_column * values[rows(start, piece), :].astype(jnp.float32)).astype(
+            jnp.bfloat16
+        )
         back_hidden = jnp.dot(scaled_part, fast[2], preferred_element_type=jnp.float32)
-        back_gate = (
-            back_hidden * pre_up * sig_gate * (1.0 + pre_gate * (1.0 - sig_gate))
-        ).astype(jnp.bfloat16)
+        back_gate = (back_hidden * slope).astype(jnp.bfloat16)
         back_up = (back_hidden * act_gate).astype(jnp.bfloat16)
-        terms = (
-            inner_rows(back_gate, key_part),
-            inner_rows(back_up, key_part),
-            inner_rows(scaled_part, hidden),
+        return (
+            lambda: inner_rows(back_gate, key_part),
+            lambda: inner_rows(back_up, key_part),
+            lambda: inner_rows(scaled_part, hidden),
         )
-        for i, term in enumerate(terms):
-            grads[i] = term if first else grads[i] + term
 
     head_copies = {}
     for half in (other, ctx):
@@ -433,21 +434,23 @@
                     {"ctx": half, "hs": depth * 4 + place},
                 )
 
-    def answer(half, step):
-        target = order[step]
-        start = half * tokens + target * step_rows
-        query_part = queries[rows(start, step_rows), :]
+    def answer(half, steps, first, amount):
+        span = rows(half * tokens + first * step_rows, step_rows * amount)
+        query_part = queries[span, :]
         query_gate = inner_cols(query_part, fresh[0])
         query_up = inner_cols(query_part, fresh[1])
         query_hidden = (query_gate * jax.nn.sigmoid(query_gate) * query_up).astype(jnp.bfloat16)
-        heads[rows(start, step_rows), :] = inner_cols(query_hidden, fresh[2]).astype(jnp.bfloat16)
-        for i in range(4):
-            if half is ctx and i == 3:
-                mixed[target, row * 2 + ctx] = heads[
-                    rows(start + inner * block_rows, block_rows), :
-                ]
-            else:
-                head_copies[half is ctx, step, i].start()
+        heads[span, :] = inner_cols(query_hidden, fresh[2]).astype(jnp.bfloat16)
+        for step in steps:
+            target = order[step]
+            for i in range(4):
+                if half is ctx and i == 3:
+                    start = half * tokens + target * step_rows
+                    mixed[target, row * 2 + ctx] = heads[
+                        rows(start + inner * block_rows, block_rows), :
+                    ]
+                else:
+                    head_copies[half is ctx, step, i].start()
 
     @pl.when(owner)
     def _():
@@ -455,22 +458,31 @@
         own_rates.wait()
         drain(lines(3 * part), ctx_recv.at[1])
         for j in range(pieces):
-            learn(ctx * tokens + j * piece, rates[ctx, :, j * piece : (j + 1) * piece], j == 0)
+            start = ctx * tokens + j * piece
+            rate = rates[ctx, :, j * piece : (j + 1) * piece]
+            for i, term in enumerate(backward(start, rate, forward(start))):
+                grads[i] = term() if j == 0 else grads[i] + term()
         start_gates(False)
         drain(rates.at[other], ctx_recv.at[0])
         for j in range(pieces):
-            drain(lines(2 * piece), ctx_recv.at[2 + j])
+            start = other * tokens + j * piece
+            drain(lines(piece), ctx_recv.at[2 + 2 * j])
+            drain(lines(piece), ctx_recv.at[3 + 2 * j])
+            made = forward(start)
             if j == pieces - 1:
                 start_gates(True)
-            learn(
-                other * tokens + j * piece, rates[other, :, j * piece : (j + 1) * piece], False
-            )
+            rate = rates[other, :, j * piece : (j + 1) * piece]
+            for i, term in enumerate(backward(start, rate, made)):
+                grads[i] = grads[i] + term()
         for i in range(3):
             fresh[i] = rescale_rows(fast[i], grads[i])
         for step in range(layers):
-            drain(lines(step_rows), ctx_recv.at[2 + pieces + step])
-            answer(other, step)
-            answer(ctx, step)
+            drain(lines(step_rows), ctx_recv.at[2 + 2 * pieces + step])
+            answer(other, [step], order[step], 1)
+            if step == 0:
+                answer(ctx, range(mid), mid - side_half, mid)
+            if step == min(1, last - 1):
+                answer(ctx, range(mid, layers), side_half, mid)
         for step in range(1, count):
             arrived((me + step) % count)
 
@@ -589,7 +601,7 @@
             pltpu.VMEM((layers, block_rows, columns), half),
             dma((5,)),
             dma((2,)),
-            dma((2 + pieces + layers,)),
+            dma((2 + 2 * pieces + layers,)),
             dma((4,)),
             dma((count,)),
             dma(()),

time: 46 us -> 45.6 us (level)
  no operation moved by 1% of the time
where the time goes in v6:
time: 45.6 us; the launch traced here: 45.4 us
  Pallas kernels  43.6 us (96%)
  local copies, waits for them, and re-layouts  1.86 us (4%)
    pallas_call x1, Pallas kernels, swapped_body(): pl.pallas_call(functools.partial(layer_kernel, layers, pieces), out_shape...  43.6 us
    transpose x1, local copies, waits for them, and re-layouts, swapped_body(): return laid.transpose(1, 0, 2)  1.86 us

profile of v6, /device:TPU:0, one launch (start us, length us, event | category | flops | bytes accessed | tf_op | source)
XLA Modules:
  0.0 45.4 jit_solution(5562717458028841310)
XLA Ops:
  0.0 43.6 %shard_map.100 = bf16[4,32,1024]{2,1,0:T(8,128)(2,1)} custom-call(bf16[1,256,512]{2,1,0:T(8,128)(2,1)} %gate_hbm.1, bf16[1,256,512]{2,1,0:T(8,128)(2,1)} %up_hbm.1, bf16[1,256,512]{2,1,0:T(8,128)(2,1)} %down_hbm.1, bf16[1,512,512]{2,1,0:T(8,128)(2,1)} %key_hbm.1, bf16[1,512,512]{2,1,0:T(8,128)(2,1)} %value_hbm.1, bf16[1,512,512]{2,1,0:T(8,128)(2,1)} %query_hbm.1, ...), custom_call_target="tpu_custom_call" | custom-call | tf_op jit(solution)/shard_map/pallas_call | solution.py:580
  43.6 1.9 %copy.11 = bf16[32,4,1024]{2,1,0:T(4,128)(2,1)} copy(bf16[32,4,1024]{2,0,1:T(8,128)(2,1)} %bitcast.2) | data formatting | bytes 524288 | tf_op jit(solution)/shard_map/transpose | solution.py:630
